TPU v7x, 32 devices: a whole 2x2x4 slice. The times are simulated.
32 devices in a mesh: img: 4 (over y, x), tpl: 8 (over z, core).
Axes of the slice: x: 2, y: 2, z: 4, core: 2. Of those that a mesh axis runs over, the one named last changes fastest.
Arguments:
- images: bfloat16 [6144, 2048], P(('img', 'tpl')), may hold values from -320 to 320
- templates: bfloat16 [3072, 2048], P('tpl'), may hold values from -0.62 to 0.62
- class_exponent: int32 [8], replicated, may hold values from 0 to 5
- class_mask: int32 [6144, 8], P('img'), may hold values from 0 to 1, as said below
Outputs:
- new_templates: float32 [3072, 2048], P('tpl', 'img')
- log_evidence: float32 [6144], P('img')
Inputs may be any that keep to these rules, and one draw needn't show every extreme that they name: `class_mask`: every image is compared with at least one class.
All inputs are finite; a program needn't handle non-finite values.
Results may differ from a plain program's by a relative error of at most 0.0023.
Values may be sent and summed in bfloat16 or wider, within the bound.
A program may use at most 64 MiB of HBM per device.

v0:
```python
import jax
import jax.numpy as jnp
from jax import lax
from jax.sharding import PartitionSpec as P

floor_score = -1e30


def per_device(images, templates, class_exponent, class_mask):
    tpl_rows = templates.shape[0]
    feature_count = templates.shape[1]
    class_count = class_exponent.shape[0]
    per_class = tpl_rows * lax.axis_size("tpl") // class_count
    global_rows = lax.axis_index("tpl") * tpl_rows + jnp.arange(tpl_rows, dtype=jnp.int32)
    owner = global_rows // per_class
    onehot = (jnp.arange(class_count, dtype=jnp.int32)[:, None] == owner[None, :]).astype(
        jnp.float32
    )
    inverse_temp = 0.5 * jnp.exp2(0.5 * class_exponent.astype(jnp.float32))
    template_beta = jnp.sum(onehot * inverse_temp[:, None], axis=0)
    allowed = jnp.dot(class_mask.astype(jnp.float32), onehot, precision=lax.Precision.HIGHEST) > 0.5
    squared_norm = jnp.sum(jnp.square(templates.astype(jnp.float32)), axis=1)
    gathered = lax.all_gather(images, "tpl", axis=0, tiled=True)
    raw = lax.dot_general(
        gathered, templates, (((1,), (1,)), ((), ())), preferred_element_type=jnp.float32
    )
    scores = template_beta[None, :] * (raw - 0.5 * squared_norm[None, :])
    local_top = jnp.max(jnp.where(allowed, scores, floor_score), axis=1)
    top = lax.pmax(local_top, "tpl")
    expo = jnp.where(allowed, jnp.exp(scores - top[:, None]), 0.0)
    totals = lax.psum(jnp.sum(expo, axis=1), "tpl")
    posterior = expo / totals[:, None]
    posterior_bf = posterior.astype(jnp.bfloat16)
    occupancy_part = jnp.sum(posterior, axis=0)
    weighted_part = lax.dot_general(
        posterior_bf, gathered, (((0,), (0,)), ((), ())), preferred_element_type=jnp.float32
    )
    columns = feature_count // lax.axis_size("img")
    col_start = lax.axis_index("img") * columns
    own_share = lax.psum_scatter(weighted_part, "img", scatter_dimension=1, tiled=True)
    occupancy = lax.psum(occupancy_part, "img")
    own_templates = lax.dynamic_slice_in_dim(templates, col_start, columns, 1).astype(jnp.float32)
    new_templates = (own_share + own_templates) / (occupancy[:, None] + 1.0)
    log_evidence = top + jnp.log(totals)
    return (new_templates, log_evidence)


def solution(mesh):
    in_specs = (P(("img", "tpl"), None), P("tpl", None), P(), P("img", None))
    out_specs = (P("tpl", "img"), P("img"))
    return jax.shard_map(
        per_device, mesh=mesh, in_specs=in_specs, out_specs=out_specs, check_vma=False
    )
```

profile of v0, /device:TPU:0, one launch (start us, length us, event | category | flops | bytes accessed | tf_op | source)
XLA Modules:
  0.0 171.4 jit_solution(5243481778394577077)
XLA Ops:
  7.2 0.0 all-gather.2.cloned.1.call-start
  7.2 0.7 all-gather.2.cloned.1.call-update
  7.9 0.0 reduce-scatter.2.cloned.1.call-start
  8.0 0.7 exponential_multiply_fusion
  8.6 0.1 select_reduce_fusion.1
  8.7 1.8 %multiply_reduce_fusion = f32[384]{0:T(512)S(1)} fusion(bf16[384,2048]{1,0:T(8,128)(2,1)} %param.5), kind=kLoop, calls=%fused_computation | loop fusion | flops 2358912 | bytes 1574400 | tf_op jit(solution)/shard_map/reduce_sum | solution.py:22
  10.5 0.0 copy-start
  10.5 66.5 %all-gather.2.cloned.1.call-done = bf16[1536,2048]{1,0:T(8,128)(2,1)} async-done(((bf16[192,2048]{1,0:T(8,128)(2,1)}), bf16[1536,2048]{1,0:T(8,128)(2,1)}) %all-gather.2.cloned.1.call-update) | async-done | bytes 6291472 | tf_op jit(solution)/shard_map/all_gather | solution.py:23
  77.1 5.2 %fusion = f32[1536,384]{0,1:T(8,128)S(1)} fusion(bf16[1536,2048]{1,0:T(8,128)(2,1)} %all-gather.2.cloned.1.call-done, bf16[384,2048]{1,0:T(8,128)(2,1)} %param.5, f32[384]{0:T(512)S(1)} %broadcast_multiply_fusion, f32[384]{0:T(512)S(1)} %select_reduce_fusion.1), kind=kOutput, calls=%fused_computation.2 | convolution fusion | flops 2417098752 | bytes 10226688 | tf_op jit(solution)/shard_map/dot_general | solution.py:24
  82.3 0.0 copy-done
  82.3 1.5 select_reduce_fusion
  83.8 14.4 %pmax.7 = f32[1536]{0:T(1024)S(1)} all-reduce(f32[1536]{0:T(1024)S(1)} %get-tuple-element.2), channel_id=1, replica_groups=mesh['img'=4,'tpl'=8] {'tpl'}, use_global_device_ids=true, to_apply=%region_3.4 | all-reduce | flops 1536 | bytes 12288 | tf_op jit(solution)/shard_map/pmax | solution.py:29
  98.3 0.6 fusion.3
  98.8 13.9 %psum.14 = f32[1536]{0:T(1024)S(1)} all-reduce(f32[1536]{0:T(1024)S(1)} %fusion.3), channel_id=1, replica_groups=mesh['img'=4,'tpl'=8] {'tpl'}, use_global_device_ids=true, to_apply=%region_5.6 | all-reduce | flops 1536 | bytes 12288 | tf_op jit(solution)/shard_map/psum | solution.py:31
  112.8 7.1 %fusion.4 = f32[384,2048]{1,0:T(8,128)} fusion(bf16[1536,2048]{1,0:T(8,128)(2,1)} %all-gather.2.cloned.1.call-done, pred[1536,384]{0,1:T(32,128)(4,1)S(1)} %get-tuple-element.3, f32[1536,384]{0,1:T(8,128)S(1)} %fusion, f32[1536]{0:T(1024)S(1)} %psum.14, f32[1536]{0:T(1024)S(1)} %pmax.7), kind=kOutput, calls=%fused_computation.9 | convolution fusion | flops 2418278400 | bytes 12398592 | tf_op jit(solution)/shard_map/dot_general | solution.py:35
  119.9 0.0 reduce-scatter.2.cloned.1.call-update
  119.9 0.7 fusion.6
  120.6 10.4 %psum.15 = f32[384]{0:T(512)S(1)} all-reduce(f32[384]{0:T(512)S(1)} %fusion.6), channel_id=1, replica_groups=mesh['img'=4,'tpl'=8] {'img'}, use_global_device_ids=true, to_apply=%region_8.9 | all-reduce | flops 384 | bytes 3072 | tf_op jit(solution)/shard_map/psum | solution.py:41
  131.0 0.6 log_add_fusion
  131.6 30.7 %reduce-scatter.2.cloned.1.call-done = f32[384,512]{1,0:T(8,128)} async-done(((f32[384,2048]{1,0:T(8,128)}), f32[384,512]{1,0:T(8,128)}) %reduce-scatter.2.cloned.1.call-update) | async-done | bytes 786448 | tf_op jit(solution)/shard_map/reduce_scatter | solution.py:40
  162.3 2.2 %add_divide_fusion = f32[384,512]{1,0:T(8,128)} fusion(f32[384,512]{1,0:T(8,128)} %reduce-scatter.2.cloned.1.call-done, f32[384]{0:T(512)S(1)} %broadcast_add_fusion, bf16[384,2048]{1,0:T(8,128)(2,1)} %param.5, s32[]{:T(128)S(6)} %select_n.22), kind=kLoop, calls=%fused_computation.11 | loop fusion | flops 589824 | bytes 1967620 | tf_op jit(solution)/shard_map/div | solution.py:43
  (3 shorter events, 0.0 us)
Async XLA Ops:
  7.2 69.9 %all-gather.2.cloned.1.call-start = ((), (), s32[]{:S(2)}) async-start(), calls=%async_computation.1 | async-start | bytes 7077888 | tf_op jit(solution)/shard_map/all_gather | solution.py:23
  7.9 154.4 %reduce-scatter.2.cloned.1.call-start = ((), (), s32[]{:S(2)}) async-start(), calls=%async_computation.2 | async-start | bytes 3932160 | tf_op jit(solution)/shard_map/reduce_scatter | solution.py:40
  10.5 71.8 %copy-start = (s32[1536,8]{0,1:T(8,128)S(1)}, s32[1536,8]{0,1:T(8,128)}, u32[]{:S(2)}) copy-start(s32[1536,8]{0,1:T(8,128)} %param.7) | copy-start | bytes 147460
Sparse Core Ops, SparseCore 0:
  9.6 67.4 all-gather.1
  120.0 42.2 reduce-scatter.1
where the time goes:
time: 172 us; the launch traced here: 171 us
  waiting for transfers between devices  97.9 us (57%)
  blocking collectives  38.7 us (23%)
  between operations  14.1 us (8%)
  matrix products  13.9 us (8%)
  other arithmetic  6.69 us (4%)
    all_gather x1, waiting for transfers between devices, per_device(): gathered = lax.all_gather(images, 'tpl', axis=0, tiled=True)  66.5 us
    reduce_scatter x1, waiting for transfers between devices, per_device(): lax.psum_scatter(weighted_part, 'img', scatter_dimension=1, tiled=True)  30.7 us
    pmax x1, blocking collectives, per_device(): top = lax.pmax(local_top, 'tpl')  14.4 us
    psum x1, blocking collectives, per_device(): totals = lax.psum(jnp.sum(expo, axis=1), 'tpl')  13.9 us
    psum x1, blocking collectives, per_device(): occupancy = lax.psum(occupancy_part, 'img')  10.4 us
    dot_general x1, matrix products, per_device(): lax.dot_general(posterior_bf, gathered, (((0,), (0,)), ((), ())), preferr...  7.11 us
    dot_general x1, matrix products, per_device(): lax.dot_general(gathered, templates, (((1,), (1,)), ((), ())), preferred_...  5.24 us
  transfers between devices with their start and end apart: 2, of which 2 were waited for; matrix products, arithmetic and copies ran while one was open for 2% of the time, Pallas kernels for 0%

commit v1 on v0

--- a/solution.py
+++ b/solution.py
@@ -20,7 +20,16 @@
     template_beta = jnp.sum(onehot * inverse_temp[:, None], axis=0)
     allowed = jnp.dot(class_mask.astype(jnp.float32), onehot, precision=lax.Precision.HIGHEST) > 0.5
     squared_norm = jnp.sum(jnp.square(templates.astype(jnp.float32)), axis=1)
-    gathered = lax.all_gather(images, "tpl", axis=0, tiled=True)
+    dev_n = lax.axis_size("tpl")
+    pieces_in = [(idx, (idx + 1) % dev_n) for idx in range(dev_n)]
+    front, block_out = ([images], [images])
+    queue = [(idx, (idx - 1) % dev_n) for idx in range(dev_n)]
+    for _ in range(dev_n // 2):
+        front.append(lax.ppermute(front[-1], "tpl", pieces_in))
+    for _ in [*range((dev_n - 1) // 2)]:
+        block_out.append(lax.ppermute(block_out[-1], "tpl", queue))
+    prior = jnp.concatenate([*front[::-1], *block_out[1:]], axis=0)
+    gathered = jnp.roll(prior, shift=(lax.axis_index("tpl") - dev_n // 2) * images.shape[0], axis=0)
     raw = lax.dot_general(
         gathered, templates, (((1,), (1,)), ((), ())), preferred_element_type=jnp.float32
     )

time: 172 us -> 187 us (1.087)
  starting transfers between devices: 0.08 us -> 11.3 us
  local copies, waits for them, and re-layouts: 0.01 us -> 9.31 us
  waiting for transfers between devices: 97.9 us -> 93.9 us
  matrix products: 13.9 us -> 11.7 us
    all_gather x1 -> x0, waiting for transfers between devices: 66.5 us -> none  [per_device(): gathered = lax.all_gather(images, 'tpl', axis=0, tiled=True)]
    ppermute x0 -> x7, waiting for transfers between devices: none -> 63.2 us  [the longest x4 63.2 us: per_device(): front.append(lax.ppermute(front[-1], 'tpl', pieces_in))]
    ppermute x0 -> x7, starting transfers between devices: none -> 11.2 us  [the longest x3 10.7 us: per_device(): block_out.append(lax.ppermute(block_out[-1], 'tpl', queue))]
    unnamed x2 -> x23, local copies, waits for them, and re-layouts: 0.01 us -> 9.24 us
    dot_general x1, matrix products: 5.24 us -> 2.66 us  [per_device(): lax.dot_general(gathered, templates, (((1,), (1,)), ((), ())), preferred_...]
  transfers between devices with their start and end apart: 2 -> 8, of which waited for: 2 -> 5; matrix products, arithmetic and copies ran while one was open for 2% -> 5% of each run, Pallas kernels for 0% -> 0%
where the time goes in v1:
time: 187 us; the launch traced here: 186 us
  waiting for transfers between devices  93.9 us (50%)
  blocking collectives  38.9 us (21%)
  between operations  14.3 us (8%)
  matrix products  11.7 us (6%)
  starting transfers between devices  11.3 us (6%)
  local copies, waits for them, and re-layouts  9.31 us (5%)
  other arithmetic  6.69 us (4%)
    ppermute x4, waiting for transfers between devices, per_device(): front.append(lax.ppermute(front[-1], 'tpl', pieces_in))  63.2 us
    reduce_scatter x1, waiting for transfers between devices, per_device(): lax.psum_scatter(weighted_part, 'img', scatter_dimension=1, tiled=True)  30.7 us
    psum x1, blocking collectives, per_device(): totals = lax.psum(jnp.sum(expo, axis=1), 'tpl')  13.9 us
    pmax x1, blocking collectives, per_device(): top = lax.pmax(local_top, 'tpl')  13.9 us
    psum x1, blocking collectives, per_device(): occupancy = lax.psum(occupancy_part, 'img')  11.1 us
    ppermute x3, starting transfers between devices, per_device(): block_out.append(lax.ppermute(block_out[-1], 'tpl', queue))  10.7 us
    unnamed x23, local copies, waits for them, and re-layouts  9.24 us
    dot_general x1, matrix products, per_device(): lax.dot_general(posterior_bf, gathered, (((0,), (0,)), ((), ())), preferr...  7.48 us
  transfers between devices with their start and end apart: 8, of which 5 were waited for; matrix products, arithmetic and copies ran while one was open for 5% of the time, Pallas kernels for 0%

profile of v1, /device:TPU:0, one launch (start us, length us, event | category | flops | bytes accessed | tf_op | source)
XLA Modules:
  0.0 186.0 jit_solution(7643583923374049066)
XLA Ops:
  7.8 13.9 %collective-permute-done = bf16[192,2048]{1,0:T(8,128)(2,1)S(1)} collective-permute-done((bf16[192,2048]{1,0:T(8,128)(2,1)}, bf16[192,2048]{1,0:T(8,128)(2,1)S(1)}, u32[]{:S(2)}, u32[]{:S(2)}) %collective-permute-start) | collective-permute-done | bytes 786464 | tf_op jit(solution)/shard_map/ppermute | solution.py:28
  21.7 3.5 %collective-permute-start.4 = (bf16[192,2048]{1,0:T(8,128)(2,1)}, bf16[192,2048]{1,0:T(8,128)(2,1)S(1)}, u32[]{:S(2)}, u32[]{:S(2)}) collective-permute-start(bf16[192,2048]{1,0:T(8,128)(2,1)} %param.4), channel_id=1, source_target_pairs={{0,7},{1,0},{2,1},{3,2},{4,3},{5,4},{6,5},{7,6},{8,15},{9,8},{10,9... | collective-permute-start | bytes 2359304 | tf_op jit(solution)/shard_map/ppermute | solution.py:30
  25.2 17.2 %collective-permute-done.1 = bf16[192,2048]{1,0:T(8,128)(2,1)S(1)} collective-permute-done((bf16[192,2048]{1,0:T(8,128)(2,1)S(1)}, bf16[192,2048]{1,0:T(8,128)(2,1)S(1)}, u32[]{:S(2)}, u32[]{:S(2)}) %collective-permute-start.1) | collective-permute-done | bytes 786464 | tf_op jit(solution)/shard_map/ppermute | solution.py:28
  42.4 3.5 %collective-permute-start.5 = (bf16[192,2048]{1,0:T(8,128)(2,1)S(1)}, bf16[192,2048]{1,0:T(8,128)(2,1)}, u32[]{:S(2)}, u32[]{:S(2)}) collective-permute-start(bf16[192,2048]{1,0:T(8,128)(2,1)S(1)} %collective-permute-done.4), channel_id=1, source_target_pairs={{0,7},{1,0},{2,1},{3,2},{4,3},{5,4},{6,5},{7,6},{8,15},{9,8},{10,9... | collective-permute-start | bytes 2359304 | tf_op jit(solution)/shard_map/ppermute | solution.py:30
  45.9 17.5 %collective-permute-done.2 = bf16[192,2048]{1,0:T(8,128)(2,1)} collective-permute-done((bf16[192,2048]{1,0:T(8,128)(2,1)S(1)}, bf16[192,2048]{1,0:T(8,128)(2,1)}, u32[]{:S(2)}, u32[]{:S(2)}) %collective-permute-start.2) | collective-permute-done | bytes 786464 | tf_op jit(solution)/shard_map/ppermute | solution.py:28
  64.2 1.8 multiply_reduce_fusion
  66.0 3.6 %collective-permute-start.6 = (bf16[192,2048]{1,0:T(8,128)(2,1)}, bf16[192,2048]{1,0:T(8,128)(2,1)S(1)}, u32[]{:S(2)}, u32[]{:S(2)}) collective-permute-start(bf16[192,2048]{1,0:T(8,128)(2,1)} %collective-permute-done.5), channel_id=1, source_target_pairs={{0,7},{1,0},{2,1},{3,2},{4,3},{5,4},{6,5},{7,6},{8,15},{9,8},{10,9... | collective-permute-start | bytes 2359304 | tf_op jit(solution)/shard_map/ppermute | solution.py:30
  69.6 14.6 %collective-permute-done.3 = bf16[192,2048]{1,0:T(8,128)(2,1)} collective-permute-done((bf16[192,2048]{1,0:T(8,128)(2,1)}, bf16[192,2048]{1,0:T(8,128)(2,1)}, u32[]{:S(2)}, u32[]{:S(2)}) %collective-permute-start.3) | collective-permute-done | bytes 786464 | tf_op jit(solution)/shard_map/ppermute | solution.py:28
  84.2 1.2 constant_dynamic-update-slice_fusion.15
  85.4 1.2 constant_dynamic-update-slice_fusion.14
  86.8 1.2 constant_dynamic-update-slice_fusion.11
  88.0 1.2 constant_dynamic-update-slice_fusion.9
  89.3 1.2 constant_dynamic-update-slice_fusion.7
  90.6 1.2 constant_dynamic-update-slice_fusion.6
  92.0 1.2 constant_dynamic-update-slice_fusion.1
  93.4 2.7 %fusion.7 = f32[1536,384]{0,1:T(8,128)S(1)} fusion(bf16[384,2048]{1,0:T(8,128)(2,1)S(1)} %copy-done.1, bf16[3072,2048]{1,0:T(8,128)(2,1)S(1)} %constant_dynamic-update-slice_fusion, s32[]{:T(128)S(6)} %select_n.34, f32[384]{0:T(512)S(1)} %broadcast_multiply_fusion, f32[384]{0:T(512)S(1)} %select_reduce_fusion.1), kind=kOutput, calls=%fused_computation.6 | convolution fusion | flops 2417098752 | bytes 10227716 | tf_op jit(solution)/shard_map/dot_general | solution.py:33
  96.0 1.5 select_reduce_fusion
  97.9 13.9 %pmax.7 = f32[1536]{0:T(1024)S(1)} all-reduce(f32[1536]{0:T(1024)S(1)} %get-tuple-element.2), channel_id=1, replica_groups=mesh['img'=4,'tpl'=8] {'tpl'}, use_global_device_ids=true, to_apply=%region_3.4 | all-reduce | flops 1536 | bytes 12288 | tf_op jit(solution)/shard_map/pmax | solution.py:38
  112.4 13.9 %psum.14 = f32[1536]{0:T(1024)S(1)} all-reduce(f32[1536]{0:T(1024)S(1)} %fusion.12), channel_id=1, replica_groups=mesh['img'=4,'tpl'=8] {'tpl'}, use_global_device_ids=true, to_apply=%region_5.6 | all-reduce | flops 1536 | bytes 12288 | tf_op jit(solution)/shard_map/psum | solution.py:40
  126.3 7.5 %fusion = f32[384,2048]{1,0:T(8,128)} fusion(bf16[3072,2048]{1,0:T(8,128)(2,1)} %copy-done.2, s32[]{:T(128)S(6)} %select_n.34, pred[1536,384]{0,1:T(32,128)(4,1)S(1)} %get-tuple-element.3, f32[1536,384]{0,1:T(8,128)S(1)} %fusion.7, f32[1536]{0:T(1024)S(1)} %psum.14, f32[1536]{0:T(1024)S(1)} %pmax.7), kind=kOutput, calls=%fused_computation | convolution fusion | flops 2418278400 | bytes 12398596 | tf_op jit(solution)/shard_map/dot_general | solution.py:44
  133.8 0.7 fusion.14
  134.5 11.1 %psum.15 = f32[384]{0:T(512)S(1)} all-reduce(f32[384]{0:T(512)S(1)} %fusion.14), channel_id=1, replica_groups=mesh['img'=4,'tpl'=8] {'img'}, use_global_device_ids=true, to_apply=%region_8.9 | all-reduce | flops 384 | bytes 3072 | tf_op jit(solution)/shard_map/psum | solution.py:50
  146.2 30.7 %reduce-scatter.2.cloned.1.call-done = f32[384,512]{1,0:T(8,128)} async-done(((f32[384,2048]{1,0:T(8,128)}), f32[384,512]{1,0:T(8,128)}) %reduce-scatter.2.cloned.1.call-update) | async-done | bytes 786448 | tf_op jit(solution)/shard_map/reduce_scatter | solution.py:49
  176.9 2.2 %add_divide_fusion = f32[384,512]{1,0:T(8,128)} fusion(f32[384,512]{1,0:T(8,128)} %reduce-scatter.2.cloned.1.call-done, f32[384]{0:T(512)S(1)} %broadcast_add_fusion, bf16[384,2048]{1,0:T(8,128)(2,1)} %param.5, s32[]{:T(128)S(6)} %select_n.37), kind=kLoop, calls=%fused_computation.14 | loop fusion | flops 589824 | bytes 1967620 | tf_op jit(solution)/shard_map/div | solution.py:52
  (33 shorter events, 3.5 us)
Async XLA Ops:
  7.2 84.7 %copy-start = (bf16[192,2048]{1,0:T(8,128)(2,1)S(1)}, bf16[192,2048]{1,0:T(8,128)(2,1)}, u32[]{:S(2)}) copy-start(bf16[192,2048]{1,0:T(8,128)(2,1)} %param.4) | copy-start | bytes 2359300
  7.2 169.7 %reduce-scatter.2.cloned.1.call-start = ((), (), s32[]{:S(2)}) async-start(), calls=%async_computation.1 | async-start | bytes 3932160 | tf_op jit(solution)/shard_map/reduce_scatter | solution.py:49
  7.2 14.5 %collective-permute-start = (bf16[192,2048]{1,0:T(8,128)(2,1)}, bf16[192,2048]{1,0:T(8,128)(2,1)S(1)}, u32[]{:S(2)}, u32[]{:S(2)}) collective-permute-start(bf16[192,2048]{1,0:T(8,128)(2,1)} %param.4), channel_id=1, source_target_pairs={{0,1},{1,2},{2,3},{3,4},{4,5},{5,6},{6,7},{7,0},{8,9},{9,10},{10,1... | collective-permute-start | bytes 2359304 | tf_op jit(solution)/shard_map/ppermute | solution.py:28
  21.7 20.7 %collective-permute-start.1 = (bf16[192,2048]{1,0:T(8,128)(2,1)S(1)}, bf16[192,2048]{1,0:T(8,128)(2,1)S(1)}, u32[]{:S(2)}, u32[]{:S(2)}) collective-permute-start(bf16[192,2048]{1,0:T(8,128)(2,1)S(1)} %collective-permute-done), channel_id=1, source_target_pairs={{0,1},{1,2},{2,3},{3,4},{4,5},{5,6},{6,7},{7,0},{8,9},{9,10},{10,1... | collective-permute-start | bytes 2359304 | tf_op jit(solution)/shard_map/ppermute | solution.py:28
  21.7 20.7 %collective-permute-start.4 = (bf16[192,2048]{1,0:T(8,128)(2,1)}, bf16[192,2048]{1,0:T(8,128)(2,1)S(1)}, u32[]{:S(2)}, u32[]{:S(2)}) collective-permute-start(bf16[192,2048]{1,0:T(8,128)(2,1)} %param.4), channel_id=1, source_target_pairs={{0,7},{1,0},{2,1},{3,2},{4,3},{5,4},{6,5},{7,6},{8,15},{9,8},{10,9... | collective-permute-start | bytes 2359304 | tf_op jit(solution)/shard_map/ppermute | solution.py:30
  42.4 21.0 %collective-permute-start.2 = (bf16[192,2048]{1,0:T(8,128)(2,1)S(1)}, bf16[192,2048]{1,0:T(8,128)(2,1)}, u32[]{:S(2)}, u32[]{:S(2)}) collective-permute-start(bf16[192,2048]{1,0:T(8,128)(2,1)S(1)} %collective-permute-done.1), channel_id=1, source_target_pairs={{0,1},{1,2},{2,3},{3,4},{4,5},{5,6},{6,7},{7,0},{8,9},{9,10},{10,1... | collective-permute-start | bytes 2359304 | tf_op jit(solution)/shard_map/ppermute | solution.py:28
  42.4 23.6 %collective-permute-start.5 = (bf16[192,2048]{1,0:T(8,128)(2,1)S(1)}, bf16[192,2048]{1,0:T(8,128)(2,1)}, u32[]{:S(2)}, u32[]{:S(2)}) collective-permute-start(bf16[192,2048]{1,0:T(8,128)(2,1)S(1)} %collective-permute-done.4), channel_id=1, source_target_pairs={{0,7},{1,0},{2,1},{3,2},{4,3},{5,4},{6,5},{7,6},{8,15},{9,8},{10,9... | collective-permute-start | bytes 2359304 | tf_op jit(solution)/shard_map/ppermute | solution.py:30
  63.4 20.8 %collective-permute-start.3 = (bf16[192,2048]{1,0:T(8,128)(2,1)}, bf16[192,2048]{1,0:T(8,128)(2,1)}, u32[]{:S(2)}, u32[]{:S(2)}) collective-permute-start(bf16[192,2048]{1,0:T(8,128)(2,1)} %collective-permute-done.2), channel_id=1, source_target_pairs={{0,1},{1,2},{2,3},{3,4},{4,5},{5,6},{6,7},{7,0},{8,9},{9,10},{10,1... | collective-permute-start | bytes 2359304 | tf_op jit(solution)/shard_map/ppermute | solution.py:28
  66.0 27.3 %copy-start.1 = (bf16[384,2048]{1,0:T(8,128)(2,1)S(1)}, bf16[384,2048]{1,0:T(8,128)(2,1)}, u32[]{:S(2)}) copy-start(bf16[384,2048]{1,0:T(8,128)(2,1)} %param.5) | copy-start | bytes 4718596
  66.0 23.2 %collective-permute-start.6 = (bf16[192,2048]{1,0:T(8,128)(2,1)}, bf16[192,2048]{1,0:T(8,128)(2,1)S(1)}, u32[]{:S(2)}, u32[]{:S(2)}) collective-permute-start(bf16[192,2048]{1,0:T(8,128)(2,1)} %collective-permute-done.5), channel_id=1, source_target_pairs={{0,7},{1,0},{2,1},{3,2},{4,3},{5,4},{6,5},{7,6},{8,15},{9,8},{10,9... | collective-permute-start | bytes 2359304 | tf_op jit(solution)/shard_map/ppermute | solution.py:30
  91.8 4.2 %copy-start.3 = (s32[1536,8]{0,1:T(8,128)S(1)}, s32[1536,8]{0,1:T(8,128)}, u32[]{:S(2)}) copy-start(s32[1536,8]{0,1:T(8,128)} %param.7) | copy-start | bytes 147460
  93.3 4.6 %copy-start.2 = (bf16[3072,2048]{1,0:T(8,128)(2,1)}, bf16[3072,2048]{1,0:T(8,128)(2,1)S(1)}, u32[]{:S(2)}) copy-start(bf16[3072,2048]{1,0:T(8,128)(2,1)S(1)} %constant_dynamic-update-slice_fusion) | copy-start | bytes 37748740
Sparse Core Ops, SparseCore 0:
  133.9 42.9 reduce-scatter.1
